TPU v7x, 1024 devices: a whole 4x8x16 slice. The times are simulated.
1024 devices in a mesh: dp: 8 (over z_lo, core), blk: 32 (over x, y), head: 4 (over z_hi).
Axes of the slice: x: 4, y: 8, z: 16 (z_hi: 4, z_lo: 4; z = z_hi * 4 + z_lo), core: 2. Of those that a mesh axis runs over, the one named last changes fastest.
Arguments:
- queries: bfloat16 [8, 16384, 4096], P('dp', ('blk', 'head')), may hold values from -8 to 8
- keys: bfloat16 [8, 16384, 512], P('dp', ('blk', 'head')), may hold values from -8 to 8
- values: bfloat16 [8, 16384, 512], P('dp', ('blk', 'head')), may hold values from -6 to 6
- lengths: int32 [8, 48], P('dp'), may hold values from 1 to 1024, 16384 in all within a row
Outputs:
- attended: bfloat16 [8, 16384, 4096], P('dp', ('blk', 'head'))
Inputs may be any that keep to these rules, and one draw needn't show every extreme that they name: `lengths`: each row sums to 16384; the longest document has exactly 1024 positions.
All inputs are finite; a program needn't handle non-finite values.
Results may differ from a plain program's by a relative error of at most 0.0035.
Values may be sent and summed in bfloat16 or wider, within the bound.
No kernel may reach another device: no remote copies, remote signals or barrier semaphores. Data moves between devices by JAX's collectives and lax.ppermute only.
A program may use at most 32 MiB of HBM per device.

v0:
```python
import jax
import jax.numpy as jnp
from jax import lax
from jax.sharding import PartitionSpec as P

HEAD_DIM = 128


def from_behind(value, axis, by):
    count = lax.axis_size(axis)
    pairs = [(i, i + by) for i in range(count) if 0 <= i + by < count]
    return lax.ppermute(value, axis, pairs)


def on_device(queries, keys, values, lengths):
    ends = jnp.cumsum(lengths[0])
    scale = 1.0 / jnp.sqrt(jnp.float32(HEAD_DIM))

    def doc_of(pos):
        return jnp.sum((pos[:, None] >= ends[None, :]).astype(jnp.int32), axis=1)

    q_heads, k_heads, v_heads = (
        lax.all_to_all(queries[0], "head", split_axis=1, concat_axis=0, tiled=True),
        lax.all_to_all(keys[0], "head", split_axis=1, concat_axis=0, tiled=True),
        lax.all_to_all(values[0], "head", split_axis=1, concat_axis=0, tiled=True),
    )
    block = q_heads.shape[0]
    width = lax.axis_size("blk")
    reach = (block * width // 16 - 1) // block + 1
    place = lax.axis_index("blk")
    block = q_heads.shape[0]
    kv_count = k_heads.shape[1] // HEAD_DIM
    group = q_heads.shape[1] // k_heads.shape[1]
    rows = jnp.arange(block, dtype=jnp.int32)
    q_pos = place * block + rows
    q_doc = doc_of(q_pos)
    query_four = q_heads.reshape(block, kv_count, group, HEAD_DIM)

    def mask_for(offset):
        k_pos = (place - offset) * block + rows
        return (
            (q_doc[:, None] == doc_of(k_pos)[None, :])
            & (k_pos[None, :] <= q_pos[:, None])
            & (k_pos[None, :] >= 0)
        )

    def attend(state, key_block, value_block, allowed):
        run_max, run_total, accum = state
        key_three = key_block.reshape(block, kv_count, HEAD_DIM)
        value_three = value_block.reshape(block, kv_count, HEAD_DIM)
        scores = (
            jnp.einsum("qhgd,khd->hgqk", query_four, key_three, preferred_element_type=jnp.float32)
            * scale
        )
        scores = jnp.where(allowed, scores, jnp.float32(-1e30))
        new_max = jnp.maximum(run_max, jnp.max(scores, axis=-1))
        correction = jnp.exp(run_max - new_max)
        expo = jnp.exp(scores - new_max[..., None])
        new_total = run_total * correction + jnp.sum(expo, axis=-1)
        added = jnp.einsum(
            "hgqk,khd->qhgd",
            expo.astype(jnp.bfloat16),
            value_three,
            preferred_element_type=jnp.float32,
        )
        new_accum = accum * jnp.transpose(correction, (2, 0, 1))[..., None] + added
        return (new_max, new_total, new_accum)

    state = (
        jnp.full((kv_count, group, block), -1e30, jnp.float32),
        jnp.zeros((kv_count, group, block), jnp.float32),
        jnp.zeros((block, kv_count, group, HEAD_DIM), jnp.float32),
    )
    state = attend(state, k_heads, v_heads, mask_for(0))
    moved = (k_heads, v_heads)
    for offset in range(1, reach + 1):
        moved = from_behind((moved[0], moved[1]), "blk", 1)
        visit_allowed = mask_for(offset)
        state = attend(state, moved[0], moved[1], visit_allowed)
    run_max, run_total, accum = state
    result = accum / jnp.transpose(run_total, (2, 0, 1))[..., None]
    result = result.reshape(block, q_heads.shape[1]).astype(jnp.bfloat16)
    returned = lax.all_to_all(result, "head", split_axis=0, concat_axis=1, tiled=True)
    return returned[None]


def solution(mesh):
    return jax.shard_map(
        on_device,
        mesh=mesh,
        in_specs=(
            P("dp", ("blk", "head"), None),
            P("dp", ("blk", "head"), None),
            P("dp", ("blk", "head"), None),
            P("dp", None),
        ),
        out_specs=P("dp", ("blk", "head"), None),
        check_vma=False,
    )
```

profile of v0, /device:TPU:174, one launch (start us, length us, event | category | flops | bytes accessed | tf_op | source)
XLA Modules:
  0.0 182.7 jit_solution(10056753144220541427)
XLA Ops:
  0.0 0.9 all_to_all.46
  0.9 0.7 copy.36
  1.6 16.9 %all-to-all-start = ((bf16[128,4,128]{2,0,1:T(8,128)(2,1)}), bf16[128,4,128]{2,0,1:T(8,128)(2,1)S(1)}, u32[]{:S(2)}, u32[]{:S(2)}) async-start(bf16[128,4,128]{2,0,1:T(8,128)(2,1)} %copy.36), calls=%async_computation | async-start | bytes 262144 | tf_op jit(solution)/shard_map/all_to_all | solution.py:24
  18.5 0.9 all_to_all.52
  19.5 0.7 copy.39
  20.1 12.9 %all-to-all-done = bf16[128,4,128]{2,0,1:T(8,128)(2,1)S(1)} async-done(((bf16[128,4,128]{2,0,1:T(8,128)(2,1)}), bf16[128,4,128]{2,0,1:T(8,128)(2,1)S(1)}, u32[]{:S(2)}, u32[]{:S(2)}) %all-to-all-start) | async-done | bytes 131104 | tf_op jit(solution)/shard_map/all_to_all | solution.py:24
  33.0 4.0 %all-to-all-start.2 = ((bf16[128,4,128]{2,0,1:T(8,128)(2,1)}), bf16[128,4,128]{2,0,1:T(8,128)(2,1)S(1)}, u32[]{:S(2)}, u32[]{:S(2)}) async-start(bf16[128,4,128]{2,0,1:T(8,128)(2,1)} %copy.39), calls=%async_computation.2 | async-start | bytes 262144 | tf_op jit(solution)/shard_map/all_to_all | solution.py:25
  37.0 1.8 %all_to_all.49 = bf16[128,4,1024]{2,1,0:T(4,128)(2,1)S(1)} reshape(bf16[1,128,4096]{2,1,0:T(8,128)(2,1)} %param.4) | data formatting | bytes 2097152 | tf_op jit(solution)/shard_map/all_to_all | solution.py:23
  38.9 1.3 copy.37
  40.2 12.1 %all-to-all-done.2 = bf16[128,4,128]{2,0,1:T(8,128)(2,1)S(1)} async-done(((bf16[128,4,128]{2,0,1:T(8,128)(2,1)}), bf16[128,4,128]{2,0,1:T(8,128)(2,1)S(1)}, u32[]{:S(2)}, u32[]{:S(2)}) %all-to-all-start.2) | async-done | bytes 131104 | tf_op jit(solution)/shard_map/all_to_all | solution.py:25
  52.3 3.5 %all-to-all-start.1 = ((bf16[128,4,1024]{2,0,1:T(8,128)(2,1)}), bf16[128,4,1024]{2,0,1:T(8,128)(2,1)S(1)}, u32[]{:S(2)}, u32[]{:S(2)}) async-start(bf16[128,4,1024]{2,0,1:T(8,128)(2,1)} %copy.37), calls=%async_computation.1 | async-start | bytes 2097152 | tf_op jit(solution)/shard_map/all_to_all | solution.py:23
  55.8 0.7 copy.35
  56.6 0.1 reduce-window.8
  56.6 0.1 reduce.6
  56.8 0.1 convert_reduce_fusion
  56.9 2.6 %collective-permute-start = (bf16[512,128]{1,0:T(8,128)(2,1)S(1)}, bf16[512,128]{1,0:T(8,128)(2,1)S(1)}, u32[]{:S(2)}, u32[]{:S(2)}) collective-permute-start(bf16[512,128]{1,0:T(8,128)(2,1)S(1)} %bitcast.205), channel_id=1, source_target_pairs={{0,4},{4,8},{8,12},{12,16},{16,20},{20,24},{24,28},{28,32},{32,36}... | collective-permute-start | bytes 393224 | tf_op jit(solution)/shard_map/ppermute | solution.py:12
  59.5 2.6 %collective-permute-start.1 = (bf16[512,128]{1,0:T(8,128)(2,1)S(1)}, bf16[512,128]{1,0:T(8,128)(2,1)S(1)}, u32[]{:S(2)}, u32[]{:S(2)}) collective-permute-start(bf16[512,128]{1,0:T(8,128)(2,1)S(1)} %bitcast.207), channel_id=1, source_target_pairs={{0,4},{4,8},{8,12},{12,16},{16,20},{20,24},{24,28},{28,32},{32,36}... | collective-permute-start | bytes 393224 | tf_op jit(solution)/shard_map/ppermute | solution.py:12
  62.1 1.1 and_and_fusion.2
  63.2 1.1 collective-permute-done
  64.3 2.6 %collective-permute-start.2 = (bf16[512,128]{1,0:T(8,128)(2,1)S(1)}, bf16[512,128]{1,0:T(8,128)(2,1)S(1)}, u32[]{:S(2)}, u32[]{:S(2)}) collective-permute-start(bf16[512,128]{1,0:T(8,128)(2,1)S(1)} %collective-permute-done), channel_id=1, source_target_pairs={{0,4},{4,8},{8,12},{12,16},{16,20},{20,24},{24,28},{28,32},{32,36}... | collective-permute-start | bytes 393224 | tf_op jit(solution)/shard_map/ppermute | solution.py:12
  66.9 0.2 collective-permute-done.1
  67.0 3.2 %collective-permute-start.3 = (bf16[512,128]{1,0:T(8,128)(2,1)S(1)}, bf16[512,128]{1,0:T(8,128)(2,1)S(1)}, u32[]{:S(2)}, u32[]{:S(2)}) collective-permute-start(bf16[512,128]{1,0:T(8,128)(2,1)S(1)} %collective-permute-done.1), channel_id=1, source_target_pairs={{0,4},{4,8},{8,12},{12,16},{16,20},{20,24},{24,28},{28,32},{32,36}... | collective-permute-start | bytes 393224 | tf_op jit(solution)/shard_map/ppermute | solution.py:12
  70.3 32.4 %all-to-all-done.1 = bf16[128,4,1024]{2,0,1:T(8,128)(2,1)S(1)} async-done(((bf16[128,4,1024]{2,0,1:T(8,128)(2,1)}), bf16[128,4,1024]{2,0,1:T(8,128)(2,1)S(1)}, u32[]{:S(2)}, u32[]{:S(2)}) %all-to-all-start.1) | async-done | bytes 1048608 | tf_op jit(solution)/shard_map/all_to_all | solution.py:23
  102.7 0.3 copy.51
  103.0 1.9 %fusion.6 = (f32[8,512]{1,0:T(8,128)S(1)}, f32[512,512,8]{1,0,2:T(8,128)S(1)}) fusion(pred[512,512]{0,1:T(8,128)(4,1)S(1)} %get-tuple-element.15, bf16[512,128,1]{1,0,2:T(8,128)(2,1)S(1)} %bitcast.206, bf16[512,8,128]{2,1,0:T(8,128)(2,1)S(1)} %bitcast.199), kind=kOutput, calls=%fused_computation.12 | convolution fusion | flops 543158272 | bytes 9846784 | tf_op jit(solution)/shard_map/qhgd,khd->hgqk/dot_general | solution.py:52
  104.9 1.9 %fusion.7 = (f32[8,512]{1,0:T(8,128)S(1)}, f32[512,512,8]{1,0,2:T(8,128)S(1)}) fusion(pred[512,512]{0,1:T(8,128)(4,1)S(1)} %get-tuple-element.17, bf16[512,8,128]{2,1,0:T(8,128)(2,1)S(1)} %bitcast.200, bf16[512,128]{1,0:T(8,128)(2,1)S(1)} %collective-permute-done), kind=kOutput, calls=%fused_computation.13 | convolution fusion | flops 543158272 | bytes 9846784 | tf_op jit(solution)/shard_map/qhgd,khd->hgqk/dot_general | solution.py:52
  106.9 0.0 collective-permute-done.2
  106.9 2.1 %fusion.8 = (f32[8,512]{1,0:T(8,128)S(1)}, f32[512,512,8]{1,0,2:T(8,128)S(1)}) fusion(pred[512,512]{0,1:T(8,128)(4,1)S(1)} %get-tuple-element.16, bf16[512,8,128]{2,1,0:T(8,128)(2,1)S(1)} %bitcast.201, bf16[512,128]{1,0:T(8,128)(2,1)S(1)} %collective-permute-done.2), kind=kOutput, calls=%fused_computation.14 | convolution fusion | flops 543158272 | bytes 9846784 | tf_op jit(solution)/shard_map/qhgd,khd->hgqk/dot_general | solution.py:52
  109.0 1.8 fusion
  110.8 3.6 %fusion.12 = f32[8,512,128]{2,1,0:T(8,128)} fusion(bf16[512,128,1]{1,0,2:T(8,128)(2,1)S(1)} %bitcast.208, f32[512,512,8]{1,0,2:T(8,128)S(1)} %get-tuple-element.23, f32[8,512]{1,0:T(8,128)S(1)} %get-tuple-element.14, pred[512,512]{0,1:T(8,128)(4,1)S(1)} %get-tuple-element.15), kind=kOutput, calls=%fused_computation.18 | convolution fusion | flops 545259520 | bytes 10895360 | tf_op jit(solution)/shard_map/hgqk,khd->qhgd/dot_general | solution.py:60
  114.4 1.8 fusion.2
  116.1 1.8 fusion.4
  117.9 0.0 copy-start
  117.9 2.2 %fusion.14 = f32[8,512,128]{2,1,0:T(8,128)S(1)} fusion(f32[512,512,8]{1,0,2:T(8,128)S(1)} %get-tuple-element.21, f32[8,512]{1,0:T(8,128)S(1)} %get-tuple-element.9, pred[512,512]{0,1:T(8,128)(4,1)S(1)} %get-tuple-element.17, bf16[512,128]{1,0:T(8,128)(2,1)S(1)} %collective-permute-done.1), kind=kOutput, calls=%fused_computation.19 | convolution fusion | flops 545259520 | bytes 10895360 | tf_op jit(solution)/shard_map/hgqk,khd->qhgd/dot_general | solution.py:60
  120.2 0.0 collective-permute-done.3
  120.2 0.0 copy-done
  120.2 4.3 %fusion.22 = bf16[512,1,8,128]{3,0,2,1:T(8,128)(2,1)S(1)} fusion(f32[8,512,128]{2,1,0:T(8,128)S(1)} %fusion.14, f32[8,512,128]{2,1,0:T(8,128)S(1)} %copy-done, f32[512,512,8]{1,0,2:T(8,128)S(1)} %get-tuple-element.19, f32[8,512]{1,0:T(8,128)S(1)} %get-tuple-element.8, pred[512,512]{0,1:T(8,128)(4,1)S(1)} %get-tuple-element.16, ...), kind=kOutput, calls=%fused_computation.26 | convolution fusion | flops 548929536 | bytes 14106624 | tf_op jit(solution)/shard_map/hgqk,khd->qhgd/dot_general | solution.py:60
  124.5 0.7 copy.45
  125.2 0.5 convert_element_type.33
  125.7 55.0 %all_to_all.61 = bf16[4,128,1024]{2,1,0:T(8,128)(2,1)S(1)} all-to-all(bf16[4,128,1024]{2,1,0:T(8,128)(2,1)S(1)} %convert_element_type.33), channel_id=1, replica_groups=mesh['dp'=8,'blk'=32,'head'=4] {'head'}, dimensions={0} | all-to-all | bytes 2097152 | tf_op jit(solution)/shard_map/all_to_all | solution.py:83
  180.7 0.7 copy.46
  181.4 1.3 copy.47
  (6 shorter events, 0.1 us)
Async XLA Ops:
  1.6 31.4 %all-to-all-start = ((bf16[128,4,128]{2,0,1:T(8,128)(2,1)}), bf16[128,4,128]{2,0,1:T(8,128)(2,1)S(1)}, u32[]{:S(2)}, u32[]{:S(2)}) async-start(bf16[128,4,128]{2,0,1:T(8,128)(2,1)} %copy.36), calls=%async_computation | async-start | bytes 262144 | tf_op jit(solution)/shard_map/all_to_all | solution.py:24
  33.0 19.2 %all-to-all-start.2 = ((bf16[128,4,128]{2,0,1:T(8,128)(2,1)}), bf16[128,4,128]{2,0,1:T(8,128)(2,1)S(1)}, u32[]{:S(2)}, u32[]{:S(2)}) async-start(bf16[128,4,128]{2,0,1:T(8,128)(2,1)} %copy.39), calls=%async_computation.2 | async-start | bytes 262144 | tf_op jit(solution)/shard_map/all_to_all | solution.py:25
  52.3 50.4 %all-to-all-start.1 = ((bf16[128,4,1024]{2,0,1:T(8,128)(2,1)}), bf16[128,4,1024]{2,0,1:T(8,128)(2,1)S(1)}, u32[]{:S(2)}, u32[]{:S(2)}) async-start(bf16[128,4,1024]{2,0,1:T(8,128)(2,1)} %copy.37), calls=%async_computation.1 | async-start | bytes 2097152 | tf_op jit(solution)/shard_map/all_to_all | solution.py:23
  56.9 7.4 %collective-permute-start = (bf16[512,128]{1,0:T(8,128)(2,1)S(1)}, bf16[512,128]{1,0:T(8,128)(2,1)S(1)}, u32[]{:S(2)}, u32[]{:S(2)}) collective-permute-start(bf16[512,128]{1,0:T(8,128)(2,1)S(1)} %bitcast.205), channel_id=1, source_target_pairs={{0,4},{4,8},{8,12},{12,16},{16,20},{20,24},{24,28},{28,32},{32,36}... | collective-permute-start | bytes 393224 | tf_op jit(solution)/shard_map/ppermute | solution.py:12
  59.5 7.5 %collective-permute-start.1 = (bf16[512,128]{1,0:T(8,128)(2,1)S(1)}, bf16[512,128]{1,0:T(8,128)(2,1)S(1)}, u32[]{:S(2)}, u32[]{:S(2)}) collective-permute-start(bf16[512,128]{1,0:T(8,128)(2,1)S(1)} %bitcast.207), channel_id=1, source_target_pairs={{0,4},{4,8},{8,12},{12,16},{16,20},{20,24},{24,28},{28,32},{32,36}... | collective-permute-start | bytes 393224 | tf_op jit(solution)/shard_map/ppermute | solution.py:12
  64.3 42.6 %collective-permute-start.2 = (bf16[512,128]{1,0:T(8,128)(2,1)S(1)}, bf16[512,128]{1,0:T(8,128)(2,1)S(1)}, u32[]{:S(2)}, u32[]{:S(2)}) collective-permute-start(bf16[512,128]{1,0:T(8,128)(2,1)S(1)} %collective-permute-done), channel_id=1, source_target_pairs={{0,4},{4,8},{8,12},{12,16},{16,20},{20,24},{24,28},{28,32},{32,36}... | collective-permute-start | bytes 393224 | tf_op jit(solution)/shard_map/ppermute | solution.py:12
  67.0 53.1 %collective-permute-start.3 = (bf16[512,128]{1,0:T(8,128)(2,1)S(1)}, bf16[512,128]{1,0:T(8,128)(2,1)S(1)}, u32[]{:S(2)}, u32[]{:S(2)}) collective-permute-start(bf16[512,128]{1,0:T(8,128)(2,1)S(1)} %collective-permute-done.1), channel_id=1, source_target_pairs={{0,4},{4,8},{8,12},{12,16},{16,20},{20,24},{24,28},{28,32},{32,36}... | collective-permute-start | bytes 393224 | tf_op jit(solution)/shard_map/ppermute | solution.py:12
  117.9 2.3 %copy-start = (f32[8,512,128]{2,1,0:T(8,128)S(1)}, f32[8,512,128]{2,1,0:T(8,128)}, u32[]{:S(2)}) copy-start(f32[8,512,128]{2,1,0:T(8,128)} %fusion.12) | copy-start | bytes 6291460
where the time goes:
time: 183 us
  waiting for transfers between devices  58.7 us (32%)
  blocking collectives  55 us (30%)
  starting transfers between devices  35.4 us (19%)
  matrix products  16.2 us (9%)
  local copies, waits for them, and re-layouts  10.5 us (6%)
  other arithmetic  6.76 us (4%)
    all_to_all x1, blocking collectives, on_device(): lax.all_to_all(result, 'head', split_axis=0, concat_axis=1, tiled=True)  55 us
    all_to_all x1, waiting for transfers between devices, on_device(): lax.all_to_all(queries[0], 'head', split_axis=1, concat_axis=0, tiled=True)  32.4 us
    all_to_all x1, starting transfers between devices, on_device(): lax.all_to_all(keys[0], 'head', split_axis=1, concat_axis=0, tiled=True)  16.9 us
    all_to_all x1, waiting for transfers between devices, on_device(): lax.all_to_all(keys[0], 'head', split_axis=1, concat_axis=0, tiled=True)  12.9 us
    all_to_all x1, waiting for transfers between devices, on_device(): lax.all_to_all(values[0], 'head', split_axis=1, concat_axis=0, tiled=True)  12.1 us
    ppermute x4, starting transfers between devices, from_behind(): return lax.ppermute(value, axis, pairs)  11 us
    dot_general x3, matrix products, attend(): jnp.einsum('hgqk,khd->qhgd', expo.astype(jnp.bfloat16), value_three, pref...  10.1 us
    dot_general x3, matrix products, attend(): jnp.einsum('qhgd,khd->hgqk', query_four, key_three, preferred_element_typ...  6.01 us
  transfers between devices with their start and end apart: 7, of which 5 were waited for; matrix products, arithmetic and copies ran while one was open for 12% of the time, Pallas kernels for 0%

commit v1 on v0

v1 whole, which is shorter than its diff:
```python
import functools
import math

import jax, jax.numpy as jnp
from jax import lax
from jax.experimental import pallas as pl
from jax.experimental.pallas import tpu as pltpu
from jax.sharding import PartitionSpec as P


HEAD_DIM = 128
NEG = -1e30

VMEM_LIMIT = 40 << 20


def doc_starts(lengths, base, rows):
    docs = lengths.shape[1]
    wide = jnp.broadcast_to(lengths.astype(jnp.float32), (docs, docs))
    r = lax.broadcasted_iota(jnp.int32, (docs, docs), 0)
    c = lax.broadcasted_iota(jnp.int32, (docs, docs), 1)
    ends = jnp.sum(jnp.where(c <= r, wide, 0.0), axis=1, keepdims=True)
    pos = (base + lax.broadcasted_iota(jnp.int32, (docs, rows), 1)).astype(jnp.float32)
    ends = jnp.broadcast_to(ends, (docs, rows))
    return jnp.max(jnp.where(ends <= pos, ends, 0.0), axis=0, keepdims=True)


def kernel(spec, chunk, first, last, where_of, group, *refs):
    n = len(spec)
    refs = list(refs)
    lengths_ref, q_ref = refs[0], refs[1]
    ks, vs = refs[2:2 + n], refs[2 + n:2 + 2 * n]
    at = 2 + 2 * n
    if not first:
        acc_in, ml_in = refs[at], refs[at + 1]
        at += 2
    if last:
        o_ref = refs[at]
        at += 1
    else:
        acc_out, ml_out = refs[at], refs[at + 1]
        at += 2
    bias_ref = refs[at]
    rows = q_ref.shape[0]
    base, starts_of = where_of(rows)

    @pl.when(pl.program_id(0) == 0)
    def _():
        start = doc_starts(lengths_ref[...], base, rows)
        key = lax.broadcasted_iota(jnp.int32, (rows, rows), 0)
        query = lax.broadcasted_iota(jnp.int32, (rows, rows), 1)
        for p in range(n):
            ok = (key + starts_of[spec[p]]).astype(jnp.float32) >= start
            if spec[p] == 0:
                ok = ok & (key <= query)
            bias_ref[p] = jnp.where(ok, 0.0, NEG)

    c = math.log2(math.e) / math.sqrt(HEAD_DIM)
    v_turned = jnp.concatenate([v[...].T for v in vs], axis=1)
    for lo in range(0, group, chunk):
        span = slice(lo * HEAD_DIM, (lo + chunk) * HEAD_DIM)
        q = jnp.concatenate([q_ref[:, (lo + t) * HEAD_DIM:(lo + t + 1) * HEAD_DIM] for t in range(chunk)], axis=0)
        scores = []
        for p in range(n):
            s = lax.dot_general(ks[p][...], q, (((1,), (1,)), ((), ())), preferred_element_type=jnp.float32)
            scores.append(s + jnp.concatenate([bias_ref[p]] * chunk, axis=1))
        top = jnp.max(functools.reduce(jnp.maximum, scores), axis=0, keepdims=True)
        if not first:
            before = ml_in[0, 0:1, span]
            top = jnp.maximum(top, before)
        weights = [jnp.exp2((s - top) * c) for s in scores]
        total = jnp.sum(functools.reduce(jnp.add, weights), axis=0, keepdims=True)
        flat = jnp.concatenate([w.astype(jnp.bfloat16) for w in weights], axis=0)
        acc = jnp.dot(v_turned, flat, preferred_element_type=jnp.float32)
        if not first:
            fix = jnp.exp2((before - top) * c)
            total = total + fix * ml_in[0, 1:2, span]
            acc = acc + fix * acc_in[0, :, span]
        if last:
            out = acc / total
            for t in range(chunk):
                o_ref[:, (lo + t) * HEAD_DIM:(lo + t + 1) * HEAD_DIM] = out[:, t * rows:(t + 1) * rows].T.astype(jnp.bfloat16)
        else:
            acc_out[0, :, span] = acc
            ml_out[0, 0:1, span] = top
            ml_out[0, 1:2, span] = total


def attend(lengths, q, pieces, state, last, where_of, chunk=2):
    rows, qw = q.shape
    kv = pieces[0][1].shape[1] // HEAD_DIM
    group = qw // HEAD_DIM // kv
    n = len(pieces)
    spec = [p[0] for p in pieces]

    def at(block):
        return pl.BlockSpec((rows, HEAD_DIM), lambda g: (block, g))

    wide = pl.BlockSpec((rows, group * HEAD_DIM), lambda g: (0, g))
    acc_spec = pl.BlockSpec((1, HEAD_DIM, group * rows), lambda g: (g, 0, 0))
    ml_spec = pl.BlockSpec((1, 2, group * rows), lambda g: (g, 0, 0))
    in_specs = [pl.BlockSpec(lengths.shape, lambda g: (0, 0)), wide]
    in_specs += [at(p[2]) for p in pieces] + [at(p[4]) for p in pieces]
    args = [lengths, q] + [p[1] for p in pieces] + [p[3] for p in pieces]
    if state is not None:
        in_specs += [acc_spec, ml_spec]
        args += list(state)
    if last:
        out_specs, out_shape = wide, jax.ShapeDtypeStruct((rows, qw), jnp.bfloat16)
    else:
        out_specs = [acc_spec, ml_spec]
        out_shape = [
            jax.ShapeDtypeStruct((kv, HEAD_DIM, group * rows), jnp.float32),
            jax.ShapeDtypeStruct((kv, 2, group * rows), jnp.float32),
        ]
    return pl.pallas_call(
        functools.partial(kernel, spec, chunk, state is None, last, where_of, group),
        grid=(kv,),
        in_specs=in_specs,
        out_specs=out_specs,
        out_shape=out_shape,
        scratch_shapes=[pltpu.VMEM((n, rows, rows), jnp.float32)],
        cost_estimate=pl.CostEstimate(
            flops=4 * n * rows * rows * qw,
            bytes_accessed=4 * rows * qw,
            transcendentals=n * rows * rows * qw // HEAD_DIM,
        ),
        compiler_params=pltpu.CompilerParams(vmem_limit_bytes=VMEM_LIMIT),
    )(*args)


NOWHERE = -(1 << 20)


def cycle(value, axis, by):
    count = lax.axis_size(axis)
    return lax.ppermute(value, axis, [(i, (i + by) % count) for i in range(count)])


def onward(value, keep):
    width, cols = lax.axis_size("blk"), lax.axis_size("head")
    pairs = [(b * cols + h, (b + 1) % width * cols + h) for b in range(width) for h in range(cols) if keep(h)]
    return lax.ppermute(value, ("blk", "head"), pairs)


def spread(value, slot):
    width, cols = lax.axis_size("blk"), lax.axis_size("head")
    pairs = []
    for b in range(width):
        for h in range(cols):
            by = 1 if (h + slot) % cols > h else -1
            pairs.append((b * cols + h, (b + by) % width * cols + h))
    return lax.ppermute(value, ("blk", "head"), pairs)


def positions(rows):
    cols = lax.axis_size("head")
    b, h = lax.axis_index("blk"), lax.axis_index("head")

    def first(row, col):
        return (row * cols + col) * rows

    at = {0: first(b, h), 1: first(b - 1, h), 2: first(b - 2, h)}
    for slot in range(1, cols):
        col = lax.rem(h + slot, cols)
        at["same", slot] = jnp.where(col < h, first(b, col), NOWHERE)
        at["one", slot] = first(b - 1, col)
        at["two", slot] = jnp.where(col > h, first(b - 2, col), NOWHERE)
        at["spread", slot] = first(jnp.where(col > h, b - 2, b), col)
    return at[0], at


def on_device(queries, keys, values, lengths):
    q = queries[0]
    own = jnp.concatenate([keys[0], values[0]], axis=0)

    def piece(kind, value):
        return (kind, value, 0, value, 1)

    left = cycle(own, "head", 1)
    right = cycle(own, "head", -1)
    below = cycle(own, "blk", 1)
    across = cycle(below, "head", 2)
    below2 = cycle(below, "blk", 1)
    left1 = cycle(left, "blk", 1)
    right1 = cycle(right, "blk", 1)
    left2 = onward(left1, lambda h: (h + 3) % 4 > h)
    right2 = onward(right1, lambda h: (h + 1) % 4 > h)
    across2 = spread(across, 2)
    first = [piece(0, own), piece(1, below), piece(2, below2), piece(("same", 3), left), piece(("same", 1), right)]
    second = [piece(("one", 3), left1), piece(("one", 1), right1), piece(("one", 2), across)]
    third = [piece(("two", 3), left2), piece(("two", 1), right2), piece(("spread", 2), across2)]
    state = attend(lengths, q, first, None, False, positions, 4)
    state = attend(lengths, q, second, state, False, positions, 4)
    return attend(lengths, q, third, state, True, positions, 4)[None]


def solution(mesh):
    return jax.shard_map(
        on_device,
        mesh=mesh,
        in_specs=(
            P("dp", ("blk", "head"), None),
            P("dp", ("blk", "head"), None),
            P("dp", ("blk", "head"), None),
            P("dp", None),
        ),
        out_specs=P("dp", ("blk", "head"), None),
        check_vma=False,
    )
```

time: 183 us -> 104 us (0.57)
  the two profiles are of different devices: /device:TPU:174 before, /device:TPU:4 now
where the time goes in v1:
time: 104 us
  starting transfers between devices  54.7 us (53%)
  waiting for transfers between devices  29.1 us (28%)
  Pallas kernels  16.9 us (16%)
  local copies, waits for them, and re-layouts  1.87 us (2%)
    ppermute x7, starting transfers between devices, cycle(): lax.ppermute(value, axis, [(i, (i + by) % count) for i in range(count)])  43 us
    ppermute x7, waiting for transfers between devices, cycle(): lax.ppermute(value, axis, [(i, (i + by) % count) for i in range(count)])  29 us
    pallas_call x3, Pallas kernels, attend(): pl.pallas_call(functools.partial(kernel, spec, chunk, state is None, last...  16.9 us
    ppermute x2, starting transfers between devices, onward(): return lax.ppermute(value, ('blk', 'head'), pairs)  8.18 us
    ppermute x1, starting transfers between devices, spread(): return lax.ppermute(value, ('blk', 'head'), pairs)  3.47 us
  transfers between devices with their start and end apart: 10, of which 2 were waited for; matrix products, arithmetic and copies ran while one was open for 0% of the time, Pallas kernels for 11%

profile of v1, /device:TPU:4, one launch (start us, length us, event | category | flops | bytes accessed | tf_op | source)
XLA Modules:
  0.0 103.7 jit_solution(14652477237670804199)
XLA Ops:
  0.0 1.0 pad_maximum_fusion.refs_2_.refs_7_
  1.0 3.5 %collective-permute-start.6 = (bf16[256,512]{1,0:T(8,128)(2,1)S(1)}, bf16[256,512]{1,0:T(8,128)(2,1)S(1)}, u32[]{:S(2)}, u32[]{:S(2)}) collective-permute-start(bf16[256,512]{1,0:T(8,128)(2,1)S(1)} %pad_maximum_fusion.refs_2_.refs_7_), channel_id=1, source_target_pairs={{0,4},{4,8},{8,12},{12,16},{16,20},{20,24},{24,28},{28,32},{32,36}... | collective-permute-start | bytes 786440 | tf_op jit(solution)/shard_map/ppermute | solution.py:137
  4.5 10.9 %collective-permute-start = (bf16[256,512]{1,0:T(8,128)(2,1)S(1)}, bf16[256,512]{1,0:T(8,128)(2,1)S(1)}, u32[]{:S(2)}, u32[]{:S(2)}) collective-permute-start(bf16[256,512]{1,0:T(8,128)(2,1)S(1)} %pad_maximum_fusion.refs_2_.refs_7_), channel_id=1, source_target_pairs={{0,1},{1,2},{2,3},{3,0},{4,5},{5,6},{6,7},{7,4},{8,9},{9,10},{10,1... | collective-permute-start | bytes 786440 | tf_op jit(solution)/shard_map/ppermute | solution.py:137
  15.4 9.2 %collective-permute-start.3 = (bf16[256,512]{1,0:T(8,128)(2,1)S(1)}, bf16[256,512]{1,0:T(8,128)(2,1)S(1)}, u32[]{:S(2)}, u32[]{:S(2)}) collective-permute-start(bf16[256,512]{1,0:T(8,128)(2,1)S(1)} %pad_maximum_fusion.refs_2_.refs_7_), channel_id=1, source_target_pairs={{0,3},{1,0},{2,1},{3,2},{4,7},{5,4},{6,5},{7,6},{8,11},{9,8},{10,9... | collective-permute-start | bytes 786440 | tf_op jit(solution)/shard_map/ppermute | solution.py:137
  24.6 0.0 collective-permute-done.6.refs_3_.refs_8_
  24.6 9.0 %collective-permute-start.7 = (bf16[256,512]{1,0:T(8,128)(2,1)S(1)}, bf16[256,512]{1,0:T(8,128)(2,1)S(1)}, u32[]{:S(2)}, u32[]{:S(2)}) collective-permute-start(bf16[256,512]{1,0:T(8,128)(2,1)S(1)} %collective-permute-done.6.refs_3_.refs_8_), channel_id=1, source_target_pairs={{0,2},{1,3},{2,0},{3,1},{4,6},{5,7},{6,4},{7,5},{8,10},{9,11},{10,... | collective-permute-start | bytes 786440 | tf_op jit(solution)/shard_map/ppermute | solution.py:137
  33.6 0.0 collective-permute-done.refs_5_.refs_10_
  33.6 3.5 %collective-permute-start.1 = (bf16[256,512]{1,0:T(8,128)(2,1)S(1)}, bf16[256,512]{1,0:T(8,128)(2,1)S(1)}, u32[]{:S(2)}, u32[]{:S(2)}) collective-permute-start(bf16[256,512]{1,0:T(8,128)(2,1)S(1)} %collective-permute-done.refs_5_.refs_10_), channel_id=1, source_target_pairs={{0,4},{4,8},{8,12},{12,16},{16,20},{20,24},{24,28},{28,32},{32,36}... | collective-permute-start | bytes 786440 | tf_op jit(solution)/shard_map/ppermute | solution.py:137
  37.1 10.5 %collective-permute-done.3.refs_6_.refs_11_ = bf16[256,512]{1,0:T(8,128)(2,1)S(1)} collective-permute-done((bf16[256,512]{1,0:T(8,128)(2,1)S(1)}, bf16[256,512]{1,0:T(8,128)(2,1)S(1)}, u32[]{:S(2)}, u32[]{:S(2)}) %collective-permute-start.3) | collective-permute-done | bytes 262176 | tf_op jit(solution)/shard_map/ppermute | solution.py:137
  47.6 3.5 %collective-permute-start.4 = (bf16[256,512]{1,0:T(8,128)(2,1)S(1)}, bf16[256,512]{1,0:T(8,128)(2,1)S(1)}, u32[]{:S(2)}, u32[]{:S(2)}) collective-permute-start(bf16[256,512]{1,0:T(8,128)(2,1)S(1)} %collective-permute-done.3.refs_6_.refs_11_), channel_id=1, source_target_pairs={{0,4},{4,8},{8,12},{12,16},{16,20},{20,24},{24,28},{28,32},{32,36}... | collective-permute-start | bytes 786440 | tf_op jit(solution)/shard_map/ppermute | solution.py:137
  51.1 3.5 %collective-permute-start.9 = (bf16[256,512]{1,0:T(8,128)(2,1)S(1)}, bf16[256,512]{1,0:T(8,128)(2,1)S(1)}, u32[]{:S(2)}, u32[]{:S(2)}) collective-permute-start(bf16[256,512]{1,0:T(8,128)(2,1)S(1)} %collective-permute-done.6.refs_3_.refs_8_), channel_id=1, source_target_pairs={{0,4},{4,8},{8,12},{12,16},{16,20},{20,24},{24,28},{28,32},{32,36}... | collective-permute-start | bytes 786440 | tf_op jit(solution)/shard_map/ppermute | solution.py:137
  54.6 18.5 %collective-permute-done.7.refs_4_.refs_7_ = bf16[256,512]{1,0:T(8,128)(2,1)S(1)} collective-permute-done((bf16[256,512]{1,0:T(8,128)(2,1)S(1)}, bf16[256,512]{1,0:T(8,128)(2,1)S(1)}, u32[]{:S(2)}, u32[]{:S(2)}) %collective-permute-start.7) | collective-permute-done | bytes 262176 | tf_op jit(solution)/shard_map/ppermute | solution.py:137
  73.1 3.5 %collective-permute-start.8 = (bf16[256,512]{1,0:T(8,128)(2,1)S(1)}, bf16[256,512]{1,0:T(8,128)(2,1)S(1)}, u32[]{:S(2)}, u32[]{:S(2)}) collective-permute-start(bf16[256,512]{1,0:T(8,128)(2,1)S(1)} %collective-permute-done.7.refs_4_.refs_7_), channel_id=1, source_target_pairs={{0,4},{1,5},{2,126},{3,127},{4,8},{5,9},{6,2},{7,3},{8,12},{9,13},... | collective-permute-start | bytes 786440 | tf_op jit(solution)/shard_map/ppermute | solution.py:153
  76.6 0.0 collective-permute-done.1.refs_2_.refs_5_
  76.6 3.5 %collective-permute-start.2 = (bf16[256,512]{1,0:T(8,128)(2,1)S(1)}, bf16[256,512]{1,0:T(8,128)(2,1)S(1)}, u32[]{:S(2)}, u32[]{:S(2)}) collective-permute-start(bf16[256,512]{1,0:T(8,128)(2,1)S(1)} %collective-permute-done.1.refs_2_.refs_5_), channel_id=1, source_target_pairs={{0,4},{4,8},{8,12},{12,16},{16,20},{20,24},{24,28},{28,32},{32,36}... | collective-permute-start | bytes 786440 | tf_op jit(solution)/shard_map/ppermute | solution.py:143
  80.1 0.0 collective-permute-done.4.refs_3_.refs_6_
  80.1 4.7 %collective-permute-start.5 = (bf16[256,512]{1,0:T(8,128)(2,1)S(1)}, bf16[256,512]{1,0:T(8,128)(2,1)S(1)}, u32[]{:S(2)}, u32[]{:S(2)}) collective-permute-start(bf16[256,512]{1,0:T(8,128)(2,1)S(1)} %collective-permute-done.4.refs_3_.refs_6_), channel_id=1, source_target_pairs={{0,4},{1,5},{2,6},{4,8},{5,9},{6,10},{8,12},{9,13},{10,14},{12,16}... | collective-permute-start | bytes 786440 | tf_op jit(solution)/shard_map/ppermute | solution.py:143
  84.8 0.0 collective-permute-done.9.refs_4_.refs_9_
  84.8 0.0 copy-start
  84.9 1.2 %copy-done = bf16[1,128,4096]{2,1,0:T(8,128)(2,1)S(1)} copy-done((bf16[1,128,4096]{2,1,0:T(8,128)(2,1)S(1)}, bf16[1,128,4096]{2,1,0:T(8,128)(2,1)}, u32[]{:S(2)}) %copy-start) | copy-done | bytes 1048600
  86.1 0.0 copy-start.1
  86.1 0.7 copy-done.1
  86.7 6.4 %shard_map.46 = (f32[4,128,1024]{2,1,0:T(8,128)S(1)}, f32[4,2,1024]{2,1,0:T(2,128)S(1)}) custom-call(s32[1,48]{1,0:T(1,128)S(1)} %copy-done.1, bf16[128,4096]{1,0:T(8,128)(2,1)S(1)} %bitcast.4, bf16[256,512]{1,0:T(8,128)(2,1)S(1)} %pad_maximum_fusion.refs_2_.refs_7_, bf16[256,512]{1,0:T(8,128)(2,1)S(1)} %collective-permute-done.6.refs_3_.refs_8_, ...), custom_call_target="tpu_custom_call" | custom-call | flops 1342177280 | bytes 2097152 | tf_op jit(solution)/shard_map/pallas_call | solution.py:116
  93.1 4.8 %shard_map.47 = (f32[4,128,1024]{2,1,0:T(8,128)S(1)}, f32[4,2,1024]{2,1,0:T(2,128)S(1)}) custom-call(s32[1,48]{1,0:T(1,128)S(1)} %copy-done.1, bf16[128,4096]{1,0:T(8,128)(2,1)S(1)} %bitcast.5, bf16[256,512]{1,0:T(8,128)(2,1)S(1)} %collective-permute-done.1.refs_2_.refs_5_, bf16[256,512]{1,0:T(8,128)(2,1)S(1)} %collective-permute-done.4.refs_3_.refs_6_, ...), custom_call_target="tpu_custom_call" | custom-call | flops 805306368 | bytes 2097152 | tf_op jit(solution)/shard_map/pallas_call | solution.py:116
  97.9 0.0 collective-permute-done.8.refs_4_.refs_7_
  97.9 0.0 collective-permute-done.2.refs_2_.refs_5_
  97.9 0.0 collective-permute-done.5.refs_3_.refs_6_
  97.9 5.7 %shard_map.48 = bf16[128,4096]{1,0:T(8,128)(2,1)} custom-call(s32[1,48]{1,0:T(1,128)S(1)} %copy-done.1, bf16[128,4096]{1,0:T(8,128)(2,1)S(1)} %bitcast.6, bf16[256,512]{1,0:T(8,128)(2,1)S(1)} %collective-permute-done.2.refs_2_.refs_5_, bf16[256,512]{1,0:T(8,128)(2,1)S(1)} %collective-permute-done.5.refs_3_.refs_6_, ...), custom_call_target="tpu_custom_call" | custom-call | flops 805306368 | bytes 2097152 | tf_op jit(solution)/shard_map/pallas_call | solution.py:116
Async XLA Ops:
  1.0 23.6 %collective-permute-start.6 = (bf16[256,512]{1,0:T(8,128)(2,1)S(1)}, bf16[256,512]{1,0:T(8,128)(2,1)S(1)}, u32[]{:S(2)}, u32[]{:S(2)}) collective-permute-start(bf16[256,512]{1,0:T(8,128)(2,1)S(1)} %pad_maximum_fusion.refs_2_.refs_7_), channel_id=1, source_target_pairs={{0,4},{4,8},{8,12},{12,16},{16,20},{20,24},{24,28},{28,32},{32,36}... | collective-permute-start | bytes 786440 | tf_op jit(solution)/shard_map/ppermute | solution.py:137
  4.5 29.1 %collective-permute-start = (bf16[256,512]{1,0:T(8,128)(2,1)S(1)}, bf16[256,512]{1,0:T(8,128)(2,1)S(1)}, u32[]{:S(2)}, u32[]{:S(2)}) collective-permute-start(bf16[256,512]{1,0:T(8,128)(2,1)S(1)} %pad_maximum_fusion.refs_2_.refs_7_), channel_id=1, source_target_pairs={{0,1},{1,2},{2,3},{3,0},{4,5},{5,6},{6,7},{7,4},{8,9},{9,10},{10,1... | collective-permute-start | bytes 786440 | tf_op jit(solution)/shard_map/ppermute | solution.py:137
  15.4 32.2 %collective-permute-start.3 = (bf16[256,512]{1,0:T(8,128)(2,1)S(1)}, bf16[256,512]{1,0:T(8,128)(2,1)S(1)}, u32[]{:S(2)}, u32[]{:S(2)}) collective-permute-start(bf16[256,512]{1,0:T(8,128)(2,1)S(1)} %pad_maximum_fusion.refs_2_.refs_7_), channel_id=1, source_target_pairs={{0,3},{1,0},{2,1},{3,2},{4,7},{5,4},{6,5},{7,6},{8,11},{9,8},{10,9... | collective-permute-start | bytes 786440 | tf_op jit(solution)/shard_map/ppermute | solution.py:137
  24.6 48.5 %collective-permute-start.7 = (bf16[256,512]{1,0:T(8,128)(2,1)S(1)}, bf16[256,512]{1,0:T(8,128)(2,1)S(1)}, u32[]{:S(2)}, u32[]{:S(2)}) collective-permute-start(bf16[256,512]{1,0:T(8,128)(2,1)S(1)} %collective-permute-done.6.refs_3_.refs_8_), channel_id=1, source_target_pairs={{0,2},{1,3},{2,0},{3,1},{4,6},{5,7},{6,4},{7,5},{8,10},{9,11},{10,... | collective-permute-start | bytes 786440 | tf_op jit(solution)/shard_map/ppermute | solution.py:137
  33.6 43.0 %collective-permute-start.1 = (bf16[256,512]{1,0:T(8,128)(2,1)S(1)}, bf16[256,512]{1,0:T(8,128)(2,1)S(1)}, u32[]{:S(2)}, u32[]{:S(2)}) collective-permute-start(bf16[256,512]{1,0:T(8,128)(2,1)S(1)} %collective-permute-done.refs_5_.refs_10_), channel_id=1, source_target_pairs={{0,4},{4,8},{8,12},{12,16},{16,20},{20,24},{24,28},{28,32},{32,36}... | collective-permute-start | bytes 786440 | tf_op jit(solution)/shard_map/ppermute | solution.py:137
  47.6 32.5 %collective-permute-start.4 = (bf16[256,512]{1,0:T(8,128)(2,1)S(1)}, bf16[256,512]{1,0:T(8,128)(2,1)S(1)}, u32[]{:S(2)}, u32[]{:S(2)}) collective-permute-start(bf16[256,512]{1,0:T(8,128)(2,1)S(1)} %collective-permute-done.3.refs_6_.refs_11_), channel_id=1, source_target_pairs={{0,4},{4,8},{8,12},{12,16},{16,20},{20,24},{24,28},{28,32},{32,36}... | collective-permute-start | bytes 786440 | tf_op jit(solution)/shard_map/ppermute | solution.py:137
  51.1 33.7 %collective-permute-start.9 = (bf16[256,512]{1,0:T(8,128)(2,1)S(1)}, bf16[256,512]{1,0:T(8,128)(2,1)S(1)}, u32[]{:S(2)}, u32[]{:S(2)}) collective-permute-start(bf16[256,512]{1,0:T(8,128)(2,1)S(1)} %collective-permute-done.6.refs_3_.refs_8_), channel_id=1, source_target_pairs={{0,4},{4,8},{8,12},{12,16},{16,20},{20,24},{24,28},{28,32},{32,36}... | collective-permute-start | bytes 786440 | tf_op jit(solution)/shard_map/ppermute | solution.py:137
  73.1 24.8 %collective-permute-start.8 = (bf16[256,512]{1,0:T(8,128)(2,1)S(1)}, bf16[256,512]{1,0:T(8,128)(2,1)S(1)}, u32[]{:S(2)}, u32[]{:S(2)}) collective-permute-start(bf16[256,512]{1,0:T(8,128)(2,1)S(1)} %collective-permute-done.7.refs_4_.refs_7_), channel_id=1, source_target_pairs={{0,4},{1,5},{2,126},{3,127},{4,8},{5,9},{6,2},{7,3},{8,12},{9,13},... | collective-permute-start | bytes 786440 | tf_op jit(solution)/shard_map/ppermute | solution.py:153
  76.6 21.3 %collective-permute-start.2 = (bf16[256,512]{1,0:T(8,128)(2,1)S(1)}, bf16[256,512]{1,0:T(8,128)(2,1)S(1)}, u32[]{:S(2)}, u32[]{:S(2)}) collective-permute-start(bf16[256,512]{1,0:T(8,128)(2,1)S(1)} %collective-permute-done.1.refs_2_.refs_5_), channel_id=1, source_target_pairs={{0,4},{4,8},{8,12},{12,16},{16,20},{20,24},{24,28},{28,32},{32,36}... | collective-permute-start | bytes 786440 | tf_op jit(solution)/shard_map/ppermute | solution.py:143
  80.1 17.8 %collective-permute-start.5 = (bf16[256,512]{1,0:T(8,128)(2,1)S(1)}, bf16[256,512]{1,0:T(8,128)(2,1)S(1)}, u32[]{:S(2)}, u32[]{:S(2)}) collective-permute-start(bf16[256,512]{1,0:T(8,128)(2,1)S(1)} %collective-permute-done.4.refs_3_.refs_6_), channel_id=1, source_target_pairs={{0,4},{1,5},{2,6},{4,8},{5,9},{6,10},{8,12},{9,13},{10,14},{12,16}... | collective-permute-start | bytes 786440 | tf_op jit(solution)/shard_map/ppermute | solution.py:143
  84.8 1.2 %copy-start = (bf16[1,128,4096]{2,1,0:T(8,128)(2,1)S(1)}, bf16[1,128,4096]{2,1,0:T(8,128)(2,1)}, u32[]{:S(2)}) copy-start(bf16[1,128,4096]{2,1,0:T(8,128)(2,1)} %param.4) | copy-start | bytes 3145732
  86.1 0.7 copy-start.1

commit v2 on v1

--- a/solution.py
+++ b/solution.py
@@ -77,9 +77,9 @@
             total = total + fix * ml_in[0, 1:2, span]
             acc = acc + fix * acc_in[0, :, span]
         if last:
-            out = acc / total
+            out = (acc * (1.0 / total)).astype(jnp.bfloat16)
             for t in range(chunk):
-                o_ref[:, (lo + t) * HEAD_DIM:(lo + t + 1) * HEAD_DIM] = out[:, t * rows:(t + 1) * rows].T.astype(jnp.bfloat16)
+                o_ref[:, (lo + t) * HEAD_DIM:(lo + t + 1) * HEAD_DIM] = out[:, t * rows:(t + 1) * rows].T
         else:
             acc_out[0, :, span] = acc
             ml_out[0, 0:1, span] = top
@@ -132,24 +132,30 @@
 NOWHERE = -(1 << 20)
 
 
-def cycle(value, axis, by):
-    count = lax.axis_size(axis)
-    return lax.ppermute(value, axis, [(i, (i + by) % count) for i in range(count)])
-
-
-def onward(value, keep):
+def around(value, by):
+    count = lax.axis_size("head")
+    return lax.ppermute(value, "head", [(h, (h + by) % count) for h in range(count)])
+
+
+def onward(value, since, into=lambda h: True):
     width, cols = lax.axis_size("blk"), lax.axis_size("head")
-    pairs = [(b * cols + h, (b + 1) % width * cols + h) for b in range(width) for h in range(cols) if keep(h)]
+    pairs = [
+        ((b - 1) % width * cols + h, b * cols + h)
+        for b in range(since, width)
+        for h in range(cols)
+        if into(h)
+    ]
     return lax.ppermute(value, ("blk", "head"), pairs)
 
 
-def spread(value, slot):
+def spread(value, by):
     width, cols = lax.axis_size("blk"), lax.axis_size("head")
     pairs = []
     for b in range(width):
         for h in range(cols):
-            by = 1 if (h + slot) % cols > h else -1
-            pairs.append((b * cols + h, (b + by) % width * cols + h))
+            step = 1 if (h + by) % cols > h else -1
+            if step < 0 or b >= 2:
+                pairs.append(((b - step) % width * cols + h, b * cols + h))
     return lax.ppermute(value, ("blk", "head"), pairs)
 
 
@@ -161,12 +167,12 @@
         return (row * cols + col) * rows
 
     at = {0: first(b, h), 1: first(b - 1, h), 2: first(b - 2, h)}
-    for slot in range(1, cols):
-        col = lax.rem(h + slot, cols)
-        at["same", slot] = jnp.where(col < h, first(b, col), NOWHERE)
-        at["one", slot] = first(b - 1, col)
-        at["two", slot] = jnp.where(col > h, first(b - 2, col), NOWHERE)
-        at["spread", slot] = first(jnp.where(col > h, b - 2, b), col)
+    for by in range(1, cols):
+        col = lax.rem(h + by, cols)
+        at["same", by] = jnp.where(col < h, first(b, col), NOWHERE)
+        at["one", by] = first(b - 1, col)
+        at["two", by] = jnp.where(col > h, first(b - 2, col), NOWHERE)
+        at["spread", by] = first(jnp.where(col > h, b - 2, b), col)
     return at[0], at
 
 
@@ -177,22 +183,25 @@
     def piece(kind, value):
         return (kind, value, 0, value, 1)
 
-    left = cycle(own, "head", 1)
-    right = cycle(own, "head", -1)
-    below = cycle(own, "blk", 1)
-    across = cycle(below, "head", 2)
-    below2 = cycle(below, "blk", 1)
-    left1 = cycle(left, "blk", 1)
-    right1 = cycle(right, "blk", 1)
-    left2 = onward(left1, lambda h: (h + 3) % 4 > h)
-    right2 = onward(right1, lambda h: (h + 1) % 4 > h)
+    left = around(own, 1)
+    right = around(own, -1)
+    below = onward(own, 0)
+    across = around(below, 2)
+    below2 = onward(below, 2)
+    left1 = onward(left, 1)
+    right1 = onward(right, 1)
+    left2 = onward(left1, 2, lambda h: (h + 3) % 4 > h)
+    right2 = onward(right1, 2, lambda h: (h + 1) % 4 > h)
     across2 = spread(across, 2)
-    first = [piece(0, own), piece(1, below), piece(2, below2), piece(("same", 3), left), piece(("same", 1), right)]
-    second = [piece(("one", 3), left1), piece(("one", 1), right1), piece(("one", 2), across)]
-    third = [piece(("two", 3), left2), piece(("two", 1), right2), piece(("spread", 2), across2)]
-    state = attend(lengths, q, first, None, False, positions, 4)
-    state = attend(lengths, q, second, state, False, positions, 4)
-    return attend(lengths, q, third, state, True, positions, 4)[None]
+    parts = (
+        ("ka", [piece(0, own), piece(1, below), piece(2, below2), piece(("same", 3), left)]),
+        ("km", [piece(("same", 1), right), piece(("one", 3), left1), piece(("one", 1), right1), piece(("one", 2), across), piece(("two", 3), left2)]),
+        ("kt", [piece(("two", 1), right2), piece(("spread", 2), across2)]),
+    )
+    state = None
+    for name, pieces in parts:
+        state = attend(lengths, q, pieces, state, name == "kt", positions, 8)
+    return state[None]
 
 
 def solution(mesh):

time: 104 us -> 98.5 us (0.947)
  the two profiles are of different devices: /device:TPU:4 before, /device:TPU:200 now
where the time goes in v2:
time: 98.5 us; the launch traced here: 98 us
  starting transfers between devices  48.9 us (50%)
  waiting for transfers between devices  31 us (31%)
  Pallas kernels  15.2 us (15%)
  local copies, waits for them, and re-layouts  1.87 us (2%)
  other arithmetic  0.99 us (1%)
    ppermute x3, waiting for transfers between devices, around(): lax.ppermute(value, 'head', [(h, (h + by) % count) for h in range(count)])  30.9 us
    ppermute x3, starting transfers between devices, around(): lax.ppermute(value, 'head', [(h, (h + by) % count) for h in range(count)])  23 us
    ppermute x6, starting transfers between devices, onward(): return lax.ppermute(value, ('blk', 'head'), pairs)  22.4 us
    pallas_call x3, Pallas kernels, attend(): pl.pallas_call(functools.partial(kernel, spec, chunk, state is None, last...  15.2 us
    ppermute x1, starting transfers between devices, spread(): return lax.ppermute(value, ('blk', 'head'), pairs)  3.48 us
  transfers between devices with their start and end apart: 10, of which 2 were waited for; matrix products, arithmetic and copies ran while one was open for 0% of the time, Pallas kernels for 11%

profile of v2, /device:TPU:200, one launch (start us, length us, event | category | flops | bytes accessed | tf_op | source)
XLA Modules:
  0.0 98.0 jit_solution(11313789574593277171)
XLA Ops:
  0.0 1.0 %pad_maximum_fusion.refs_2_.refs_6_ = bf16[256,512]{1,0:T(8,128)(2,1)S(1)} fusion(bf16[128,512]{1,0:T(8,128)(2,1)} %bitcast.7, bf16[128,512]{1,0:T(8,128)(2,1)} %bitcast.8), kind=kLoop, calls=%fused_computation | loop fusion | flops 524288 | bytes 524288 | tf_op jit(solution)/shard_map/concatenate | solution.py:181
  1.0 10.9 %collective-permute-start.6 = (bf16[256,512]{1,0:T(8,128)(2,1)S(1)}, bf16[256,512]{1,0:T(8,128)(2,1)S(1)}, u32[]{:S(2)}, u32[]{:S(2)}) collective-permute-start(bf16[256,512]{1,0:T(8,128)(2,1)S(1)} %pad_maximum_fusion.refs_2_.refs_6_), channel_id=1, source_target_pairs={{0,1},{1,2},{2,3},{3,0},{4,5},{5,6},{6,7},{7,4},{8,9},{9,10},{10,1... | collective-permute-start | bytes 786440 | tf_op jit(solution)/shard_map/ppermute | solution.py:137
  11.9 3.5 %collective-permute-start.3 = (bf16[256,512]{1,0:T(8,128)(2,1)S(1)}, bf16[256,512]{1,0:T(8,128)(2,1)S(1)}, u32[]{:S(2)}, u32[]{:S(2)}) collective-permute-start(bf16[256,512]{1,0:T(8,128)(2,1)S(1)} %pad_maximum_fusion.refs_2_.refs_6_), channel_id=1, source_target_pairs={{124,0},{125,1},{126,2},{127,3},{0,4},{1,5},{2,6},{3,7},{4,8},{5,9... | collective-permute-start | bytes 786440 | tf_op jit(solution)/shard_map/ppermute | solution.py:148
  15.4 6.5 %collective-permute-start = (bf16[256,512]{1,0:T(8,128)(2,1)S(1)}, bf16[256,512]{1,0:T(8,128)(2,1)S(1)}, u32[]{:S(2)}, u32[]{:S(2)}) collective-permute-start(bf16[256,512]{1,0:T(8,128)(2,1)S(1)} %pad_maximum_fusion.refs_2_.refs_6_), channel_id=1, source_target_pairs={{0,3},{1,0},{2,1},{3,2},{4,7},{5,4},{6,5},{7,6},{8,11},{9,8},{10,9... | collective-permute-start | bytes 786440 | tf_op jit(solution)/shard_map/ppermute | solution.py:137
  21.9 17.7 %collective-permute-done.6.refs_5_.refs_9_ = bf16[256,512]{1,0:T(8,128)(2,1)S(1)} collective-permute-done((bf16[256,512]{1,0:T(8,128)(2,1)S(1)}, bf16[256,512]{1,0:T(8,128)(2,1)S(1)}, u32[]{:S(2)}, u32[]{:S(2)}) %collective-permute-start.6) | collective-permute-done | bytes 262176 | tf_op jit(solution)/shard_map/ppermute | solution.py:137
  39.6 3.5 %collective-permute-start.7 = (bf16[256,512]{1,0:T(8,128)(2,1)S(1)}, bf16[256,512]{1,0:T(8,128)(2,1)S(1)}, u32[]{:S(2)}, u32[]{:S(2)}) collective-permute-start(bf16[256,512]{1,0:T(8,128)(2,1)S(1)} %collective-permute-done.6.refs_5_.refs_9_), channel_id=1, source_target_pairs={{0,4},{1,5},{2,6},{3,7},{4,8},{5,9},{6,10},{7,11},{8,12},{9,13},{1... | collective-permute-start | bytes 786440 | tf_op jit(solution)/shard_map/ppermute | solution.py:148
  43.1 0.0 collective-permute-done.3.refs_3_.refs_7_
  43.1 5.6 %collective-permute-start.4 = (bf16[256,512]{1,0:T(8,128)(2,1)S(1)}, bf16[256,512]{1,0:T(8,128)(2,1)S(1)}, u32[]{:S(2)}, u32[]{:S(2)}) collective-permute-start(bf16[256,512]{1,0:T(8,128)(2,1)S(1)} %collective-permute-done.3.refs_3_.refs_7_), channel_id=1, source_target_pairs={{0,2},{1,3},{2,0},{3,1},{4,6},{5,7},{6,4},{7,5},{8,10},{9,11},{10,... | collective-permute-start | bytes 786440 | tf_op jit(solution)/shard_map/ppermute | solution.py:137
  48.7 0.0 collective-permute-done.refs_2_.refs_7_
  48.7 3.5 %collective-permute-start.1 = (bf16[256,512]{1,0:T(8,128)(2,1)S(1)}, bf16[256,512]{1,0:T(8,128)(2,1)S(1)}, u32[]{:S(2)}, u32[]{:S(2)}) collective-permute-start(bf16[256,512]{1,0:T(8,128)(2,1)S(1)} %collective-permute-done.refs_2_.refs_7_), channel_id=1, source_target_pairs={{0,4},{1,5},{2,6},{3,7},{4,8},{5,9},{6,10},{7,11},{8,12},{9,13},{1... | collective-permute-start | bytes 786440 | tf_op jit(solution)/shard_map/ppermute | solution.py:148
  52.2 4.7 %collective-permute-start.9 = (bf16[256,512]{1,0:T(8,128)(2,1)S(1)}, bf16[256,512]{1,0:T(8,128)(2,1)S(1)}, u32[]{:S(2)}, u32[]{:S(2)}) collective-permute-start(bf16[256,512]{1,0:T(8,128)(2,1)S(1)} %collective-permute-done.3.refs_3_.refs_7_), channel_id=1, source_target_pairs={{4,8},{5,9},{6,10},{7,11},{8,12},{9,13},{10,14},{11,15},{12,16},{1... | collective-permute-start | bytes 786440 | tf_op jit(solution)/shard_map/ppermute | solution.py:148
  56.9 0.0 collective-permute-done.7.refs_3_.refs_8_
  56.9 2.6 %collective-permute-start.8 = (bf16[256,512]{1,0:T(8,128)(2,1)S(1)}, bf16[256,512]{1,0:T(8,128)(2,1)S(1)}, u32[]{:S(2)}, u32[]{:S(2)}) collective-permute-start(bf16[256,512]{1,0:T(8,128)(2,1)S(1)} %collective-permute-done.7.refs_3_.refs_8_), channel_id=1, source_target_pairs={{4,8},{8,12},{12,16},{16,20},{20,24},{24,28},{28,32},{32,36},{36,4... | collective-permute-start | bytes 786440 | tf_op jit(solution)/shard_map/ppermute | solution.py:148
  59.5 13.2 %collective-permute-done.4.refs_5_.refs_10_ = bf16[256,512]{1,0:T(8,128)(2,1)S(1)} collective-permute-done((bf16[256,512]{1,0:T(8,128)(2,1)S(1)}, bf16[256,512]{1,0:T(8,128)(2,1)S(1)}, u32[]{:S(2)}, u32[]{:S(2)}) %collective-permute-start.4) | collective-permute-done | bytes 262176 | tf_op jit(solution)/shard_map/ppermute | solution.py:137
  72.7 3.5 %collective-permute-start.5 = (bf16[256,512]{1,0:T(8,128)(2,1)S(1)}, bf16[256,512]{1,0:T(8,128)(2,1)S(1)}, u32[]{:S(2)}, u32[]{:S(2)}) collective-permute-start(bf16[256,512]{1,0:T(8,128)(2,1)S(1)} %collective-permute-done.4.refs_5_.refs_10_), channel_id=1, source_target_pairs={{6,2},{7,3},{10,6},{11,7},{4,8},{5,9},{14,10},{15,11},{8,12},{9,13... | collective-permute-start | bytes 786440 | tf_op jit(solution)/shard_map/ppermute | solution.py:159
  76.2 0.0 collective-permute-done.1.refs_4_.refs_9_
  76.3 4.7 %collective-permute-start.2 = (bf16[256,512]{1,0:T(8,128)(2,1)S(1)}, bf16[256,512]{1,0:T(8,128)(2,1)S(1)}, u32[]{:S(2)}, u32[]{:S(2)}) collective-permute-start(bf16[256,512]{1,0:T(8,128)(2,1)S(1)} %collective-permute-done.1.refs_4_.refs_9_), channel_id=1, source_target_pairs={{4,8},{5,9},{6,10},{8,12},{9,13},{10,14},{12,16},{13,17},{14,18},{... | collective-permute-start | bytes 786440 | tf_op jit(solution)/shard_map/ppermute | solution.py:148
  81.0 0.0 collective-permute-done.9.refs_4_.refs_8_
  81.0 0.0 copy-start
  81.0 1.2 %copy-done = bf16[1,128,4096]{2,1,0:T(8,128)(2,1)S(1)} copy-done((bf16[1,128,4096]{2,1,0:T(8,128)(2,1)S(1)}, bf16[1,128,4096]{2,1,0:T(8,128)(2,1)}, u32[]{:S(2)}) %copy-start) | copy-done | bytes 1048600
  82.2 0.0 copy-start.1
  82.2 0.7 copy-done.1
  82.8 5.0 %shard_map.46 = (f32[4,128,1024]{2,1,0:T(8,128)S(1)}, f32[4,2,1024]{2,1,0:T(2,128)S(1)}) custom-call(s32[1,48]{1,0:T(1,128)S(1)} %copy-done.1, bf16[128,4096]{1,0:T(8,128)(2,1)S(1)} %bitcast.4, bf16[256,512]{1,0:T(8,128)(2,1)S(1)} %pad_maximum_fusion.refs_2_.refs_6_, bf16[256,512]{1,0:T(8,128)(2,1)S(1)} %collective-permute-done.3.refs_3_.refs_7_, ...), custom_call_target="tpu_custom_call" | custom-call | flops 1073741824 | bytes 2097152 | tf_op jit(solution)/shard_map/pallas_call | solution.py:116
  87.8 0.0 collective-permute-done.8.refs_6_.refs_11_
  87.8 6.1 %shard_map.47 = (f32[4,128,1024]{2,1,0:T(8,128)S(1)}, f32[4,2,1024]{2,1,0:T(2,128)S(1)}) custom-call(s32[1,48]{1,0:T(1,128)S(1)} %copy-done.1, bf16[128,4096]{1,0:T(8,128)(2,1)S(1)} %bitcast.5, bf16[256,512]{1,0:T(8,128)(2,1)S(1)} %collective-permute-done.refs_2_.refs_7_, bf16[256,512]{1,0:T(8,128)(2,1)S(1)} %collective-permute-done.7.refs_3_.refs_8_, ...), custom_call_target="tpu_custom_call" | custom-call | flops 1342177280 | bytes 2097152 | tf_op jit(solution)/shard_map/pallas_call | solution.py:116
  93.9 0.0 collective-permute-done.5.refs_3_.refs_5_
  93.9 0.0 collective-permute-done.2.refs_2_.refs_4_
  93.9 4.1 %shard_map.48 = bf16[128,4096]{1,0:T(8,128)(2,1)} custom-call(s32[1,48]{1,0:T(1,128)S(1)} %copy-done.1, bf16[128,4096]{1,0:T(8,128)(2,1)S(1)} %bitcast.6, bf16[256,512]{1,0:T(8,128)(2,1)S(1)} %collective-permute-done.2.refs_2_.refs_4_, bf16[256,512]{1,0:T(8,128)(2,1)S(1)} %collective-permute-done.5.refs_3_.refs_5_, ...), custom_call_target="tpu_custom_call" | custom-call | flops 536870912 | bytes 2097152 | tf_op jit(solution)/shard_map/pallas_call | solution.py:116
Async XLA Ops:
  1.0 38.6 %collective-permute-start.6 = (bf16[256,512]{1,0:T(8,128)(2,1)S(1)}, bf16[256,512]{1,0:T(8,128)(2,1)S(1)}, u32[]{:S(2)}, u32[]{:S(2)}) collective-permute-start(bf16[256,512]{1,0:T(8,128)(2,1)S(1)} %pad_maximum_fusion.refs_2_.refs_6_), channel_id=1, source_target_pairs={{0,1},{1,2},{2,3},{3,0},{4,5},{5,6},{6,7},{7,4},{8,9},{9,10},{10,1... | collective-permute-start | bytes 786440 | tf_op jit(solution)/shard_map/ppermute | solution.py:137
  11.9 31.2 %collective-permute-start.3 = (bf16[256,512]{1,0:T(8,128)(2,1)S(1)}, bf16[256,512]{1,0:T(8,128)(2,1)S(1)}, u32[]{:S(2)}, u32[]{:S(2)}) collective-permute-start(bf16[256,512]{1,0:T(8,128)(2,1)S(1)} %pad_maximum_fusion.refs_2_.refs_6_), channel_id=1, source_target_pairs={{124,0},{125,1},{126,2},{127,3},{0,4},{1,5},{2,6},{3,7},{4,8},{5,9... | collective-permute-start | bytes 786440 | tf_op jit(solution)/shard_map/ppermute | solution.py:148
  15.4 33.3 %collective-permute-start = (bf16[256,512]{1,0:T(8,128)(2,1)S(1)}, bf16[256,512]{1,0:T(8,128)(2,1)S(1)}, u32[]{:S(2)}, u32[]{:S(2)}) collective-permute-start(bf16[256,512]{1,0:T(8,128)(2,1)S(1)} %pad_maximum_fusion.refs_2_.refs_6_), channel_id=1, source_target_pairs={{0,3},{1,0},{2,1},{3,2},{4,7},{5,4},{6,5},{7,6},{8,11},{9,8},{10,9... | collective-permute-start | bytes 786440 | tf_op jit(solution)/shard_map/ppermute | solution.py:137
  39.6 17.3 %collective-permute-start.7 = (bf16[256,512]{1,0:T(8,128)(2,1)S(1)}, bf16[256,512]{1,0:T(8,128)(2,1)S(1)}, u32[]{:S(2)}, u32[]{:S(2)}) collective-permute-start(bf16[256,512]{1,0:T(8,128)(2,1)S(1)} %collective-permute-done.6.refs_5_.refs_9_), channel_id=1, source_target_pairs={{0,4},{1,5},{2,6},{3,7},{4,8},{5,9},{6,10},{7,11},{8,12},{9,13},{1... | collective-permute-start | bytes 786440 | tf_op jit(solution)/shard_map/ppermute | solution.py:148
  43.1 29.7 %collective-permute-start.4 = (bf16[256,512]{1,0:T(8,128)(2,1)S(1)}, bf16[256,512]{1,0:T(8,128)(2,1)S(1)}, u32[]{:S(2)}, u32[]{:S(2)}) collective-permute-start(bf16[256,512]{1,0:T(8,128)(2,1)S(1)} %collective-permute-done.3.refs_3_.refs_7_), channel_id=1, source_target_pairs={{0,2},{1,3},{2,0},{3,1},{4,6},{5,7},{6,4},{7,5},{8,10},{9,11},{10,... | collective-permute-start | bytes 786440 | tf_op jit(solution)/shard_map/ppermute | solution.py:137
  48.7 27.6 %collective-permute-start.1 = (bf16[256,512]{1,0:T(8,128)(2,1)S(1)}, bf16[256,512]{1,0:T(8,128)(2,1)S(1)}, u32[]{:S(2)}, u32[]{:S(2)}) collective-permute-start(bf16[256,512]{1,0:T(8,128)(2,1)S(1)} %collective-permute-done.refs_2_.refs_7_), channel_id=1, source_target_pairs={{0,4},{1,5},{2,6},{3,7},{4,8},{5,9},{6,10},{7,11},{8,12},{9,13},{1... | collective-permute-start | bytes 786440 | tf_op jit(solution)/shard_map/ppermute | solution.py:148
  52.2 28.8 %collective-permute-start.9 = (bf16[256,512]{1,0:T(8,128)(2,1)S(1)}, bf16[256,512]{1,0:T(8,128)(2,1)S(1)}, u32[]{:S(2)}, u32[]{:S(2)}) collective-permute-start(bf16[256,512]{1,0:T(8,128)(2,1)S(1)} %collective-permute-done.3.refs_3_.refs_7_), channel_id=1, source_target_pairs={{4,8},{5,9},{6,10},{7,11},{8,12},{9,13},{10,14},{11,15},{12,16},{1... | collective-permute-start | bytes 786440 | tf_op jit(solution)/shard_map/ppermute | solution.py:148
  56.9 30.9 %collective-permute-start.8 = (bf16[256,512]{1,0:T(8,128)(2,1)S(1)}, bf16[256,512]{1,0:T(8,128)(2,1)S(1)}, u32[]{:S(2)}, u32[]{:S(2)}) collective-permute-start(bf16[256,512]{1,0:T(8,128)(2,1)S(1)} %collective-permute-done.7.refs_3_.refs_8_), channel_id=1, source_target_pairs={{4,8},{8,12},{12,16},{16,20},{20,24},{24,28},{28,32},{32,36},{36,4... | collective-permute-start | bytes 786440 | tf_op jit(solution)/shard_map/ppermute | solution.py:148
  72.7 21.2 %collective-permute-start.5 = (bf16[256,512]{1,0:T(8,128)(2,1)S(1)}, bf16[256,512]{1,0:T(8,128)(2,1)S(1)}, u32[]{:S(2)}, u32[]{:S(2)}) collective-permute-start(bf16[256,512]{1,0:T(8,128)(2,1)S(1)} %collective-permute-done.4.refs_5_.refs_10_), channel_id=1, source_target_pairs={{6,2},{7,3},{10,6},{11,7},{4,8},{5,9},{14,10},{15,11},{8,12},{9,13... | collective-permute-start | bytes 786440 | tf_op jit(solution)/shard_map/ppermute | solution.py:159
  76.3 17.7 %collective-permute-start.2 = (bf16[256,512]{1,0:T(8,128)(2,1)S(1)}, bf16[256,512]{1,0:T(8,128)(2,1)S(1)}, u32[]{:S(2)}, u32[]{:S(2)}) collective-permute-start(bf16[256,512]{1,0:T(8,128)(2,1)S(1)} %collective-permute-done.1.refs_4_.refs_9_), channel_id=1, source_target_pairs={{4,8},{5,9},{6,10},{8,12},{9,13},{10,14},{12,16},{13,17},{14,18},{... | collective-permute-start | bytes 786440 | tf_op jit(solution)/shard_map/ppermute | solution.py:148
  81.0 1.2 %copy-start = (bf16[1,128,4096]{2,1,0:T(8,128)(2,1)S(1)}, bf16[1,128,4096]{2,1,0:T(8,128)(2,1)}, u32[]{:S(2)}) copy-start(bf16[1,128,4096]{2,1,0:T(8,128)(2,1)} %param.4) | copy-start | bytes 3145732
  82.2 0.7 copy-start.1
